TPU v7x, 32 devices: a whole 2x2x4 slice. The times are simulated.
32 devices in a mesh: au: 8 (over z, core), vert: 4 (over y, x).
Axes of the slice: x: 2, y: 2, z: 4, core: 2. Of those that a mesh axis runs over, the one named last changes fastest.
Arguments:
- vis_value: float32 [128, 128, 2, 128], P('au', 'vert'), may hold values from -6 to 6
- vis_pos: int32 [128, 128, 2, 128], P('au', 'vert'), may hold values from 0 to 1048575, as said below
- counts: int32 [128, 128], P('au', 'vert'), may hold values from 21 to 128, as said below
- kernel: float32 [8, 128], replicated, may hold values from 0.05 to 0.5
Outputs:
- image: float32 [8192, 8192], P(('au', 'vert'))
Inputs may be any that keep to these rules, and one draw needn't show every extreme that they name: Slot k of patch (p, q) holds a visibility exactly when k < counts[p, q]; in every draw some patch has all 128 slots live. vis_pos[p, q, 0, k] lies in [p * 64 * 128, (p + 1) * 64 * 128) and vis_pos[p, q, 1, k] in [q * 64 * 128, (q + 1) * 64 * 128), in every slot.
All inputs are finite; a program needn't handle non-finite values.
Results may differ from a plain program's by a relative error of at most 0.0003.
Values sent between devices are 32-bit elements; how exact they have to be, the bound alone decides.
A program may use at most 192 MiB of HBM per device.

v0:
```python
import math
import jax
import jax.numpy as jnp
from jax import lax
from jax.sharding import PartitionSpec as P

PATCH = 64
PR = 128
PC = 128
highest = lax.Precision.HIGH


def passed_along(value, axis, steps):
    count = lax.axis_size(axis)
    initial, last = (max(0, -steps), min(count, count - steps))
    return lax.ppermute(value, axis, [(source, source + steps) for source in range(initial, last)])


def fourier(length):
    index_list = jnp.arange(length, dtype=jnp.int32)
    angles = (
        2.0
        * math.pi
        / length
        * (index_list[:, None] * index_list[None, :] % length).astype(jnp.float32)
    )
    return jnp.stack([jnp.cos(angles), jnp.sin(angles)])


def twiddle(outer_size, inner_size, length):
    row_index = jnp.arange(outer_size, dtype=jnp.int32)[:, None]
    col_index = jnp.arange(inner_size, dtype=jnp.int32)[None, :]
    angles = 2.0 * math.pi / length * (row_index * col_index % length).astype(jnp.float32)
    return (jnp.cos(angles), jnp.sin(angles))


def complex_table(length):
    cos, sin = fourier(length)
    return jnp.stack([jnp.stack([cos, -sin]), jnp.stack([sin, cos])])


def row_transform(field):
    band_count, outer_size, _, rows, inner_size = field.shape
    length = outer_size * inner_size
    turn_cos, turn_sin = twiddle(outer_size, inner_size, length)
    product = jnp.einsum("scaq,bqcip->sbiap", complex_table(outer_size), field, precision=highest)
    rotated = jnp.stack(
        [
            product[0] * turn_cos - product[1] * turn_sin,
            product[0] * turn_sin + product[1] * turn_cos,
        ]
    )
    result = jnp.einsum("scyp,cbiap->sbiya", complex_table(inner_size), rotated, precision=highest)
    return result.reshape(2, band_count * rows, length)


def column_transform(received, image_scale):
    length = received.shape[1]
    item_count = received.shape[3]
    inner_size = 128
    outer_size = length // inner_size
    turn_cos, turn_sin = twiddle(outer_size, inner_size, length)
    blocked = received.reshape(2, outer_size, inner_size, item_count)
    product = jnp.einsum("scaq,cqpy->sapy", complex_table(outer_size), blocked, precision=highest)
    turn_cos = turn_cos[..., None]
    turn_sin = turn_sin[..., None]
    rotated = jnp.stack(
        [
            product[0] * turn_cos - product[1] * turn_sin,
            product[0] * turn_sin + product[1] * turn_cos,
        ]
    )
    last_table = complex_table(inner_size)[0] * image_scale
    image_rows = jnp.einsum("cbp,capy->yba", last_table, rotated, precision=highest)
    return image_rows.reshape(item_count, length)


def joined(array, group):
    count, lead, slots = array.shape
    blocks = array.reshape(count // group, group, lead, slots)
    before = jnp.roll(blocks[:, group - 1], 1, axis=0)
    return jnp.concatenate([before] + [blocks[:, step] for step in range(group)], axis=-1)


def spread(distance, taps):
    weights = jnp.zeros(distance.shape, jnp.float32)
    for tap_step in range(taps.shape[1]):
        weights = jnp.where(distance == tap_step, taps[:, tap_step][:, None], weights)
    return weights


def band_tiles(values, positions, counts, kernel):
    kernel_width, oversample = kernel.shape
    column_count, _, slot_count = values.shape
    width = 128
    group = width // PATCH
    group_count = column_count // group
    live_mask = jnp.arange(slot_count, dtype=jnp.int32)[None, :] < counts[:, None]
    cell_index = positions // oversample
    fine_index = positions - cell_index * oversample
    selector = (
        fine_index[:, :, None, :] == jnp.arange(oversample, dtype=jnp.int32)[:, None]
    ).astype(jnp.float32)
    taps = jnp.einsum("to,naok->natk", kernel, selector, precision=highest)
    taps = joined(taps.reshape(column_count, 2 * kernel_width, slot_count), group)
    cells = joined(cell_index, group)
    scaled = joined(jnp.where(live_mask[:, None], values, 0.0), group)
    extent = PATCH + kernel_width
    row_distance = (
        jnp.arange(extent, dtype=jnp.int32)[None, :, None] - (cells[:, 0] % PATCH)[:, None]
    )
    starts = jnp.arange(group_count, dtype=jnp.int32) * width
    columns = starts[:, None] + jnp.arange(width, dtype=jnp.int32)
    column_distance = columns[:, :, None] - cells[:, 1][:, None]
    row_weights = spread(row_distance, taps[:, :kernel_width])
    column_weights = spread(column_distance, taps[:, kernel_width:])
    scaled_rows = scaled[:, :, None] * row_weights[:, None]
    return jnp.einsum("mcik,mjk->mcij", scaled_rows, column_weights, precision=highest)


def local(vis_value, vis_pos, counts, kernel):
    kernel_width = kernel.shape[0]
    device_count = lax.axis_size("au") * lax.axis_size("vert")
    slot_count = vis_value.shape[3]
    image_scale = 1.0 / math.sqrt(PR * PC * slot_count)
    vert_count = lax.axis_size("vert")
    band_count = vis_value.shape[0] // vert_count
    local_columns = vis_value.shape[1]
    moved_values = lax.all_to_all(
        vis_value.reshape(vert_count, band_count, local_columns, 2, slot_count),
        "vert",
        split_axis=0,
        concat_axis=2,
        tiled=True,
    )
    positions, tallies = (
        lax.all_to_all(
            vis_pos.reshape(vert_count, band_count, local_columns, 2, slot_count),
            "vert",
            split_axis=0,
            concat_axis=2,
            tiled=True,
        ),
        lax.all_to_all(
            counts.reshape(vert_count, band_count, local_columns),
            "vert",
            split_axis=0,
            concat_axis=2,
            tiled=True,
        ),
    )
    column_count = local_columns * vert_count
    values = moved_values.reshape(band_count, column_count, 2, slot_count)
    positions = positions.reshape(band_count, column_count, 2, slot_count)
    tallies = tallies.reshape(band_count, column_count)
    tiles = lax.map(lambda members: band_tiles(*members, kernel), (values, positions, tallies))
    spill = tiles[..., PATCH:, :]
    arrived = passed_along(spill[-1], ("au", "vert"), 1)
    above = jnp.concatenate([arrived[None], spill[:-1]], axis=0)
    field = jnp.concatenate(
        [tiles[..., :kernel_width, :] + above, tiles[..., kernel_width:PATCH, :]], axis=3
    )
    row_field = row_transform(field)
    length = row_field.shape[2]
    column_share = length // device_count
    return column_transform(
        lax.all_to_all(
            row_field.reshape(2, row_field.shape[1], device_count, column_share),
            ("au", "vert"),
            split_axis=2,
            concat_axis=1,
            tiled=True,
        ),
        image_scale,
    )


def solution(mesh):
    in_specs = (P("au", "vert", None, None), P("au", "vert", None, None), P("au", "vert"), P())
    out_specs = P(("au", "vert"), None)
    return jax.shard_map(local, mesh=mesh, in_specs=in_specs, out_specs=out_specs, check_vma=False)
```

profile of v0, /device:TPU:0, one launch (start us, length us, event | category | flops | bytes accessed | tf_op | source)
XLA Modules:
  0.0 784.5 jit_solution(12170232325561670538)
XLA Ops:
  1.4 5.2 all-to-all-start
  6.5 1.9 copy.110
  8.4 2.8 all-to-all-done
  11.2 3.5 all-to-all-start.1
  14.7 1.9 copy.112
  16.6 4.8 all-to-all-done.1
  21.4 3.5 all-to-all-start.2
  27.8 3.6 all-to-all-done.2
  31.5 147.3 %while.12 = (s32[]{:T(128)}, f32[4,64,2,72,128]{4,1,2,3,0:T(8,128)}, s32[4,128]{1,0:T(4,128)S(1)}, f32[4,128,2,128]{3,1,2,0:T(8,128)S(1)}, s32[4,128,2,128]{3,1,2,0:T(8,128)S(1)}, /*index=5*/f32[8,128]{1,0:T(8,128)}, s32[]{:T(128)}) while((s32[]{:T(128)}, f32[4,64,2,72,128]{4,1,2,3,0:T(8,128)}, s32[4,128]{1,0:T(4,128)S(1)}, ...), condition=%wide.region_1.2_spmd, body=%wide.region_0.1_spmd.sunk | while | flops 3013378048 | bytes 48205400 | solution.py:156
  31.7 4.8 fusion.141
  36.8 1.4 fusion.142
  38.9 6.2 select_select_fusion.2
  46.1 18.5 %fusion.147 = f32[1,64,2,72,128]{4,3,2,1,0:T(8,128)S(1)} fusion(f32[64,384]{1,0:T(8,128)S(1)} %get-tuple-element.238, f32[64,384]{1,0:T(8,128)S(1)} %get-tuple-element.239, f32[64,384]{1,0:T(8,128)S(1)} %get-tuple-element.242, f32[64,384]{1,0:T(8,128)S(1)} %get-tuple-element.243, f32[64,384]{1,0:T(8,128)S(1)} %get-tuple-element.246, ...), kind=kOutput, calls=%fused_computation.54.clone.1 | convolution fusion | flops 2774925312 | bytes 12910592 | tf_op jit(solution)/shard_map/while/body/eval_jaxpr/mcik,mjk->mcij/dot_general | solution.py:118
  64.7 3.6 copy_dynamic-update-slice_fusion.2
  68.4 4.8 fusion.141
  73.5 1.4 fusion.142
  75.6 6.2 select_select_fusion.2
  82.8 18.5 %fusion.147 = f32[1,64,2,72,128]{4,3,2,1,0:T(8,128)S(1)} fusion(f32[64,384]{1,0:T(8,128)S(1)} %get-tuple-element.238, f32[64,384]{1,0:T(8,128)S(1)} %get-tuple-element.239, f32[64,384]{1,0:T(8,128)S(1)} %get-tuple-element.242, f32[64,384]{1,0:T(8,128)S(1)} %get-tuple-element.243, f32[64,384]{1,0:T(8,128)S(1)} %get-tuple-element.246, ...), kind=kOutput, calls=%fused_computation.54.clone.1 | convolution fusion | flops 2774925312 | bytes 12910592 | tf_op jit(solution)/shard_map/while/body/eval_jaxpr/mcik,mjk->mcij/dot_general | solution.py:118
  101.4 3.6 copy_dynamic-update-slice_fusion.2
  105.2 4.8 fusion.141
  110.3 1.4 fusion.142
  112.3 6.2 select_select_fusion.2
  119.6 18.5 %fusion.147 = f32[1,64,2,72,128]{4,3,2,1,0:T(8,128)S(1)} fusion(f32[64,384]{1,0:T(8,128)S(1)} %get-tuple-element.238, f32[64,384]{1,0:T(8,128)S(1)} %get-tuple-element.239, f32[64,384]{1,0:T(8,128)S(1)} %get-tuple-element.242, f32[64,384]{1,0:T(8,128)S(1)} %get-tuple-element.243, f32[64,384]{1,0:T(8,128)S(1)} %get-tuple-element.246, ...), kind=kOutput, calls=%fused_computation.54.clone.1 | convolution fusion | flops 2774925312 | bytes 12910592 | tf_op jit(solution)/shard_map/while/body/eval_jaxpr/mcik,mjk->mcij/dot_general | solution.py:118
  138.1 3.7 copy_dynamic-update-slice_fusion.2
  142.0 4.8 fusion.141
  147.1 1.4 fusion.142
  149.1 6.2 select_select_fusion.2
  156.3 18.5 %fusion.147 = f32[1,64,2,72,128]{4,3,2,1,0:T(8,128)S(1)} fusion(f32[64,384]{1,0:T(8,128)S(1)} %get-tuple-element.238, f32[64,384]{1,0:T(8,128)S(1)} %get-tuple-element.239, f32[64,384]{1,0:T(8,128)S(1)} %get-tuple-element.242, f32[64,384]{1,0:T(8,128)S(1)} %get-tuple-element.243, f32[64,384]{1,0:T(8,128)S(1)} %get-tuple-element.246, ...), kind=kOutput, calls=%fused_computation.54.clone.1 | convolution fusion | flops 2774925312 | bytes 12910592 | tf_op jit(solution)/shard_map/while/body/eval_jaxpr/mcik,mjk->mcij/dot_general | solution.py:118
  174.9 3.6 copy_dynamic-update-slice_fusion.2
  179.9 3.4 collective-permute-start
  184.0 1.5 slice.264
  185.6 13.6 %slice.265 = f32[4,64,2,56,128]{4,1,2,3,0:T(8,128)} slice(f32[4,64,2,72,128]{4,1,2,3,0:T(8,128)} %get-tuple-element.85), slice={[0:4], [0:64], [0:2], [8:64], [0:128]} | slice | bytes 29360128 | tf_op jit(solution)/shard_map/slice | solution.py:161
  199.1 2.0 maximum_add_fusion
  201.1 13.5 %fusion.77 = f32[2,4,64,64,128]{4,3,0,2,1:T(8,128)} fusion(f32[4,64,2,56,128]{4,1,2,3,0:T(8,128)} %slice.265, f32[4,64,2,8,128]{4,1,2,3,0:T(8,128)S(1)} %maximum_add_fusion, f32[1,2,64,64]{3,2,1,0:T(8,128)S(1)} %get-tuple-element.147, f32[1,2,64,64]{3,2,1,0:T(8,128)S(1)} %get-tuple-element.146), kind=kOutput, calls=%fused_computation.136 | convolution fusion | flops 3225436160 | bytes 33619968 | tf_op jit(solution)/shard_map/scaq,bqcip->sbiap/dot_general | solution.py:46
  214.6 9.8 %multiply_subtract_fusion.1 = (f32[1,4,64,64,128]{4,3,0,2,1:T(8,128)S(1)}, f32[1,4,64,64,128]{4,3,0,2,1:T(8,128)}) fusion(f32[2,4,64,64,128]{4,3,0,2,1:T(8,128)} %fusion.77, f32[64,128]{1,0:T(8,128)S(1)} %copy-done, f32[64,128]{1,0:T(8,128)S(1)} %copy-done.1), kind=kLoop, calls=%fused_computation.140 | loop fusion | flops 12582912 | bytes 33619968 | tf_op jit(solution)/shard_map/sub | solution.py:49
  224.4 12.7 %fusion.76 = f32[2,4,64,128,64]{3,4,0,2,1:T(8,128)} fusion(f32[1,4,64,64,128]{4,3,0,2,1:T(8,128)} %get-tuple-element.143, f32[1,4,64,64,128]{4,3,0,2,1:T(8,128)S(1)} %get-tuple-element.142, f32[1,2,128,128]{3,2,1,0:T(8,128)S(1)} %get-tuple-element.145, f32[1,2,128,128]{3,2,1,0:T(8,128)S(1)} %get-tuple-element.144), kind=kOutput, calls=%fused_computation.135 | convolution fusion | flops 6446710784 | bytes 33816576 | tf_op jit(solution)/shard_map/scyp,cbiap->sbiya/dot_general | solution.py:53
  237.1 23.0 %copy.118 = f32[2,4,64,128,64]{4,3,2,1,0:T(8,128)} copy(f32[2,4,64,128,64]{3,4,0,2,1:T(8,128)} %fusion.76) | data formatting | bytes 33554432 | tf_op jit(solution)/shard_map/scyp,cbiap->sbiya/transpose | solution.py:53
  260.1 27.9 %reshape_reshape.3 = f32[2,256,32,256]{3,2,1,0:T(8,128)} reshape(f32[2,4,64,128,64]{4,3,2,1,0:T(8,128)} %copy.118) | data formatting | bytes 33554432 | tf_op jit(solution)/shard_map/reshape;reshape | solution.py:168
  288.0 15.9 %copy.119 = f32[2,256,32,256]{3,1,0,2:T(8,128)} copy(f32[2,256,32,256]{3,2,1,0:T(8,128)} %reshape_reshape.3) | data formatting | bytes 33554432 | tf_op jit(solution)/shard_map/reshape;reshape | solution.py:168
  303.9 5.2 all-to-all-start.3
  309.3 382.5 %all-to-all-done.3 = f32[2,256,32,256]{3,1,0,2:T(8,128)} async-done(((f32[2,256,32,256]{3,1,0,2:T(8,128)}), f32[2,256,32,256]{3,1,0,2:T(8,128)}, u32[]{:S(2)}, u32[]{:S(2)}) %all-to-all-start.3) | async-done | bytes 16777248 | tf_op jit(solution)/shard_map/all_to_all | solution.py:167
  691.8 11.5 %copy.120 = f32[2,256,32,256]{3,1,2,0:T(8,128)} copy(f32[2,256,32,256]{3,1,0,2:T(8,128)} %all-to-all-done.3) | data formatting | bytes 33554432 | tf_op jit(solution)/shard_map/all_to_all | solution.py:167
  703.3 25.6 %fusion.78 = f32[2,64,128,256]{3,1,2,0:T(8,128)} fusion(f32[2,64,128,256]{3,2,1,0:T(8,128)} %bitcast.254, f32[1,2,64,64]{3,2,1,0:T(8,128)S(1)} %get-tuple-element.147, f32[1,2,64,64]{3,2,1,0:T(8,128)S(1)} %get-tuple-element.146), kind=kOutput, calls=%fused_computation.141 | convolution fusion | flops 3221241856 | bytes 33619968 | tf_op jit(solution)/shard_map/scaq,cqpy->sapy/dot_general | solution.py:64
  728.9 13.8 %multiply_subtract_fusion = (f32[1,64,128,256]{3,1,2,0:T(8,128)}, f32[1,64,128,256]{3,1,2,0:T(8,128)}) fusion(f32[2,64,128,256]{3,1,2,0:T(8,128)} %fusion.78, f32[64,128]{0,1:T(8,128)S(1)} %copy.123, f32[64,128]{0,1:T(8,128)S(1)} %copy.122), kind=kLoop, calls=%fused_computation.138 | loop fusion | flops 12582912 | bytes 33619968 | tf_op jit(solution)/shard_map/sub | solution.py:69
  742.7 6.5 pad_maximum_fusion.2
  749.2 14.5 %fusion.81 = f32[256,128,64]{0,1,2:T(8,128)} fusion(f32[2,64,128,256]{3,1,2,0:T(8,128)S(1)} %pad_maximum_fusion.2, f32[1,128,128]{2,1,0:T(8,128)S(1)} %fusion.112, f32[1,128,128]{2,1,0:T(8,128)S(1)} %get-tuple-element.153), kind=kOutput, calls=%fused_computation.142 | convolution fusion | flops 3221291008 | bytes 25296896 | tf_op jit(solution)/shard_map/cbp,capy->yba/dot_general | solution.py:74
  763.7 11.5 %copy.125 = f32[256,128,64]{0,2,1:T(8,128)} copy(f32[256,128,64]{0,1,2:T(8,128)} %fusion.81) | data formatting | bytes 16777216 | tf_op jit(solution)/shard_map/cbp,capy->yba/transpose | solution.py:74
  775.2 8.9 %copy.126 = f32[256,8192]{1,0:T(8,128)} copy(f32[256,8192]{0,1:T(8,128)} %bitcast.258) | data formatting | bytes 16777216 | tf_op jit(solution)/shard_map/reshape | solution.py:75
  (164 shorter events, 13.9 us)
Async XLA Ops:
  1.4 9.9 %all-to-all-start = ((s32[4,1,128]{2,1,0:T(1,128)}), s32[4,1,128]{2,1,0:T(1,128)S(1)}, u32[]{:S(2)}, u32[]{:S(2)}) async-start(s32[4,1,128]{2,1,0:T(1,128)} %reshape.440), calls=%async_computation | async-start | bytes 4096 | tf_op jit(solution)/shard_map/all_to_all | solution.py:144
  11.2 10.2 %all-to-all-start.1 = ((f32[4,4,32,2,128]{4,2,3,1,0:T(8,128)}), f32[4,4,32,2,128]{4,2,3,1,0:T(8,128)S(1)}, u32[]{:S(2)}, u32[]{:S(2)}) async-start(f32[4,4,32,2,128]{4,2,3,1,0:T(8,128)} %bitcast.32), calls=%async_computation.1 | async-start | bytes 1048576 | tf_op jit(solution)/shard_map/all_to_all | solution.py:129
  21.4 10.0 %all-to-all-start.2 = ((s32[4,4,32,2,128]{4,2,3,1,0:T(8,128)}), s32[4,4,32,2,128]{4,2,3,1,0:T(8,128)S(1)}, u32[]{:S(2)}, u32[]{:S(2)}) async-start(s32[4,4,32,2,128]{4,2,3,1,0:T(8,128)} %bitcast.36), calls=%async_computation.2 | async-start | bytes 1048576 | tf_op jit(solution)/shard_map/all_to_all | solution.py:137
  31.5 152.5 %copy-start.2 = (f32[1,64,64]{2,1,0:T(8,128)S(1)}, f32[1,64,64]{2,1,0:T(8,128)}, u32[]{:S(2)}) copy-start(f32[1,64,64]{2,1,0:T(8,128)} %get-tuple-element.148) | copy-start | bytes 49156
  31.5 152.5 %copy-start.3 = (f32[1,64,64]{2,1,0:T(8,128)S(1)}, f32[1,64,64]{2,1,0:T(8,128)}, u32[]{:S(2)}) copy-start(f32[1,64,64]{2,1,0:T(8,128)} %get-tuple-element.149) | copy-start | bytes 49156
  179.9 19.3 %collective-permute-start = (f32[64,2,8,128]{3,0,1,2:T(8,128)S(1)}, f32[64,2,8,128]{3,0,1,2:T(8,128)S(1)}, u32[]{:S(2)}, u32[]{:S(2)}) collective-permute-start(f32[64,2,8,128]{3,0,1,2:T(8,128)S(1)} %slice_bitcast_fusion.7), channel_id=1, source_target_pairs={{0,1},{1,2},{2,3},{3,4},{4,5},{5,6},{6,7},{7,8},{8,9},{9,10},{10,1... | collective-permute-start | bytes 1572872 | tf_op jit(solution)/shard_map/ppermute | solution.py:16
  201.1 13.5 %copy-start = (f32[64,128]{1,0:T(8,128)S(1)}, f32[64,128]{1,0:T(8,128)}, u32[]{:S(2)}) copy-start(f32[64,128]{1,0:T(8,128)} %get-tuple-element.150) | copy-start | bytes 98308
  201.1 13.5 %copy-start.1 = (f32[64,128]{1,0:T(8,128)S(1)}, f32[64,128]{1,0:T(8,128)}, u32[]{:S(2)}) copy-start(f32[64,128]{1,0:T(8,128)} %get-tuple-element.151) | copy-start | bytes 98308
  303.9 387.9 %all-to-all-start.3 = ((f32[2,256,32,256]{3,1,0,2:T(8,128)}), f32[2,256,32,256]{3,1,0,2:T(8,128)}, u32[]{:S(2)}, u32[]{:S(2)}) async-start(f32[2,256,32,256]{3,1,0,2:T(8,128)} %copy.119), calls=%async_computation.3 | async-start | bytes 33554432 | tf_op jit(solution)/shard_map/all_to_all | solution.py:167
where the time goes:
time: 796 us; the launch traced here: 784 us
  waiting for transfers between devices  394 us (49%)
  matrix products  160 us (20%)
  local copies, waits for them, and re-layouts  145 us (18%)
  other arithmetic  63.3 us (8%)
  starting transfers between devices  20.7 us (3%)
    all_to_all x1, waiting for transfers between devices, local(): lax.all_to_all(row_field.reshape(2, row_field.shape[1], device_count, col...  382 us
    dot_general x4, matrix products, band_tiles(): jnp.einsum('mcik,mjk->mcij', scaled_rows, column_weights, precision=highest)  74.2 us
    another operation x2, local copies, waits for them, and re-layouts, local(): row_field.reshape(2, row_field.shape[1], device_count, column_share)  43.8 us
    dot_general x1, matrix products, column_transform(): jnp.einsum('scaq,cqpy->sapy', complex_table(outer_size), blocked, precisi...  25.6 us
    select_n x4, other arithmetic, spread(): jnp.where(distance == tap_step, taps[:, tap_step][:, None], weights)  24.8 us
    transpose x1, local copies, waits for them, and re-layouts, row_transform(): jnp.einsum('scyp,cbiap->sbiya', complex_table(inner_size), rotated, preci...  23 us
    dot_general x4, matrix products, band_tiles(): taps = jnp.einsum('to,naok->natk', kernel, selector, precision=highest)  19.3 us
  transfers between devices with their start and end apart: 5, of which 4 were waited for; matrix products, arithmetic and copies ran while one was open for 3% of the time, Pallas kernels for 0%

commit v1 on v0

--- a/solution.py
+++ b/solution.py
@@ -164,12 +164,20 @@
     length = row_field.shape[2]
     column_share = length // device_count
     return column_transform(
-        lax.all_to_all(
-            row_field.reshape(2, row_field.shape[1], device_count, column_share),
-            ("au", "vert"),
-            split_axis=2,
-            concat_axis=1,
-            tiled=True,
+        jnp.concatenate(
+            lax.all_to_all(
+                jnp.stack(
+                    jnp.split(
+                        row_field.reshape(2, row_field.shape[1], device_count, column_share),
+                        lax.axis_size(("au", "vert")),
+                        axis=2,
+                    )
+                ),
+                ("au", "vert"),
+                0,
+                0,
+            ),
+            axis=1,
         ),
         image_scale,
     )

time: 796 us -> 892 us (1.12)
  local copies, waits for them, and re-layouts: 145 us -> 241 us
    unnamed x12 -> x43, local copies, waits for them, and re-layouts: 5.28 us -> 112 us
    another operation x2 -> x1, local copies, waits for them, and re-layouts: 43.8 us -> 28.3 us  [local(): row_field.reshape(2, row_field.shape[1], device_count, column_share)]
    reshape x0 -> x1, local copies, waits for them, and re-layouts: none -> 12.7 us  [local(): jnp.concatenate(lax.all_to_all(jnp.stack(jnp.split(row_field.reshape(2, r...]
    all_to_all x1 -> x0, local copies, waits for them, and re-layouts: 11.5 us -> none  [local(): lax.all_to_all(row_field.reshape(2, row_field.shape[1], device_count, col...]
where the time goes in v1:
time: 892 us; the launch traced here: 880 us
  waiting for transfers between devices  394 us (44%)
  local copies, waits for them, and re-layouts  241 us (27%)
  matrix products  159 us (18%)
  other arithmetic  63.5 us (7%)
  starting transfers between devices  20.6 us (2%)
    all_to_all x1, waiting for transfers between devices, local(): lax.all_to_all(jnp.stack(jnp.split(row_field.reshape(2, row_field.shape[1...  382 us
    unnamed x43, local copies, waits for them, and re-layouts  112 us
    dot_general x4, matrix products, band_tiles(): jnp.einsum('mcik,mjk->mcij', scaled_rows, column_weights, precision=highest)  74.2 us
    another operation x1, local copies, waits for them, and re-layouts, local(): row_field.reshape(2, row_field.shape[1], device_count, column_share)  28.3 us
    dot_general x1, matrix products, column_transform(): jnp.einsum('scaq,cqpy->sapy', complex_table(outer_size), blocked, precisi...  25.6 us
    select_n x4, other arithmetic, spread(): jnp.where(distance == tap_step, taps[:, tap_step][:, None], weights)  24.8 us
    transpose x1, local copies, waits for them, and re-layouts, row_transform(): jnp.einsum('scyp,cbiap->sbiya', complex_table(inner_size), rotated, preci...  23 us
    dot_general x4, matrix products, band_tiles(): taps = jnp.einsum('to,naok->natk', kernel, selector, precision=highest)  19.3 us
  transfers between devices with their start and end apart: 5, of which 4 were waited for; matrix products, arithmetic and copies ran while one was open for 3% of the time, Pallas kernels for 0%

profile of v1, /device:TPU:0, one launch (start us, length us, event | category | flops | bytes accessed | tf_op | source)
XLA Modules:
  0.0 879.6 jit_solution(4348975563565421045)
XLA Ops:
  1.4 5.2 all-to-all-start
  11.2 3.5 all-to-all-start.1
  16.6 4.8 all-to-all-done.1
  21.4 3.5 all-to-all-start.2
  27.8 3.6 all-to-all-done.2
  31.5 147.1 %while.12 = (s32[]{:T(128)}, f32[4,64,2,72,128]{4,1,2,3,0:T(8,128)}, s32[4,128]{1,0:T(4,128)S(1)}, f32[4,128,2,128]{3,1,2,0:T(8,128)S(1)}, s32[4,128,2,128]{3,1,2,0:T(8,128)S(1)}, /*index=5*/f32[8,128]{1,0:T(8,128)}, s32[]{:T(128)}) while((s32[]{:T(128)}, f32[4,64,2,72,128]{4,1,2,3,0:T(8,128)}, s32[4,128]{1,0:T(4,128)S(1)}, ...), condition=%wide.region_1.2_spmd, body=%wide.region_0.1_spmd.sunk | while | flops 3013378048 | bytes 48205400 | solution.py:156
  31.7 4.8 fusion.173
  38.9 6.2 select_select_fusion.2
  46.1 18.5 %fusion.179 = f32[1,64,2,72,128]{4,3,2,1,0:T(8,128)S(1)} fusion(f32[64,384]{1,0:T(8,128)S(1)} %get-tuple-element.238, f32[64,384]{1,0:T(8,128)S(1)} %get-tuple-element.239, f32[64,384]{1,0:T(8,128)S(1)} %get-tuple-element.242, f32[64,384]{1,0:T(8,128)S(1)} %get-tuple-element.243, f32[64,384]{1,0:T(8,128)S(1)} %get-tuple-element.246, ...), kind=kOutput, calls=%fused_computation.54.clone.1 | convolution fusion | flops 2774925312 | bytes 12910592 | tf_op jit(solution)/shard_map/while/body/eval_jaxpr/mcik,mjk->mcij/dot_general | solution.py:118
  64.6 3.6 copy_dynamic-update-slice_fusion.2
  68.4 4.8 fusion.173
  75.6 6.2 select_select_fusion.2
  82.8 18.5 %fusion.179 = f32[1,64,2,72,128]{4,3,2,1,0:T(8,128)S(1)} fusion(f32[64,384]{1,0:T(8,128)S(1)} %get-tuple-element.238, f32[64,384]{1,0:T(8,128)S(1)} %get-tuple-element.239, f32[64,384]{1,0:T(8,128)S(1)} %get-tuple-element.242, f32[64,384]{1,0:T(8,128)S(1)} %get-tuple-element.243, f32[64,384]{1,0:T(8,128)S(1)} %get-tuple-element.246, ...), kind=kOutput, calls=%fused_computation.54.clone.1 | convolution fusion | flops 2774925312 | bytes 12910592 | tf_op jit(solution)/shard_map/while/body/eval_jaxpr/mcik,mjk->mcij/dot_general | solution.py:118
  101.4 3.6 copy_dynamic-update-slice_fusion.2
  105.2 4.8 fusion.173
  112.3 6.2 select_select_fusion.2
  119.6 18.5 %fusion.179 = f32[1,64,2,72,128]{4,3,2,1,0:T(8,128)S(1)} fusion(f32[64,384]{1,0:T(8,128)S(1)} %get-tuple-element.238, f32[64,384]{1,0:T(8,128)S(1)} %get-tuple-element.239, f32[64,384]{1,0:T(8,128)S(1)} %get-tuple-element.242, f32[64,384]{1,0:T(8,128)S(1)} %get-tuple-element.243, f32[64,384]{1,0:T(8,128)S(1)} %get-tuple-element.246, ...), kind=kOutput, calls=%fused_computation.54.clone.1 | convolution fusion | flops 2774925312 | bytes 12910592 | tf_op jit(solution)/shard_map/while/body/eval_jaxpr/mcik,mjk->mcij/dot_general | solution.py:118
  138.1 3.7 copy_dynamic-update-slice_fusion.2
  142.0 4.8 fusion.173
  149.1 6.2 select_select_fusion.2
  156.3 18.5 %fusion.179 = f32[1,64,2,72,128]{4,3,2,1,0:T(8,128)S(1)} fusion(f32[64,384]{1,0:T(8,128)S(1)} %get-tuple-element.238, f32[64,384]{1,0:T(8,128)S(1)} %get-tuple-element.239, f32[64,384]{1,0:T(8,128)S(1)} %get-tuple-element.242, f32[64,384]{1,0:T(8,128)S(1)} %get-tuple-element.243, f32[64,384]{1,0:T(8,128)S(1)} %get-tuple-element.246, ...), kind=kOutput, calls=%fused_computation.54.clone.1 | convolution fusion | flops 2774925312 | bytes 12910592 | tf_op jit(solution)/shard_map/while/body/eval_jaxpr/mcik,mjk->mcij/dot_general | solution.py:118
  174.9 3.6 copy_dynamic-update-slice_fusion.2
  185.4 13.6 %slice.265 = f32[4,64,2,56,128]{4,1,2,3,0:T(8,128)} slice(f32[4,64,2,72,128]{4,1,2,3,0:T(8,128)} %get-tuple-element.85), slice={[0:4], [0:64], [0:2], [8:64], [0:128]} | slice | bytes 29360128 | tf_op jit(solution)/shard_map/slice | solution.py:161
  201.0 13.5 %fusion.77 = f32[2,4,64,64,128]{4,3,0,2,1:T(8,128)} fusion(f32[4,64,2,56,128]{4,1,2,3,0:T(8,128)} %slice.265, f32[4,64,2,8,128]{4,1,2,3,0:T(8,128)S(1)} %maximum_add_fusion, f32[1,2,64,64]{3,2,1,0:T(8,128)S(1)} %get-tuple-element.147, f32[1,2,64,64]{3,2,1,0:T(8,128)S(1)} %get-tuple-element.146), kind=kOutput, calls=%fused_computation.136 | convolution fusion | flops 3225436160 | bytes 33619968 | tf_op jit(solution)/shard_map/scaq,bqcip->sbiap/dot_general | solution.py:46
  214.5 9.8 %multiply_subtract_fusion.1 = (f32[1,4,64,64,128]{4,3,0,2,1:T(8,128)S(1)}, f32[1,4,64,64,128]{4,3,0,2,1:T(8,128)}) fusion(f32[2,4,64,64,128]{4,3,0,2,1:T(8,128)} %fusion.77, f32[64,128]{1,0:T(8,128)S(1)} %copy-done, f32[64,128]{1,0:T(8,128)S(1)} %copy-done.1), kind=kLoop, calls=%fused_computation.140 | loop fusion | flops 12582912 | bytes 33619968 | tf_op jit(solution)/shard_map/sub | solution.py:49
  224.3 12.7 %fusion.76 = f32[2,4,64,128,64]{3,4,0,2,1:T(8,128)} fusion(f32[1,4,64,64,128]{4,3,0,2,1:T(8,128)} %get-tuple-element.143, f32[1,4,64,64,128]{4,3,0,2,1:T(8,128)S(1)} %get-tuple-element.142, f32[1,2,128,128]{3,2,1,0:T(8,128)S(1)} %get-tuple-element.145, f32[1,2,128,128]{3,2,1,0:T(8,128)S(1)} %get-tuple-element.144), kind=kOutput, calls=%fused_computation.135 | convolution fusion | flops 6446710784 | bytes 33816576 | tf_op jit(solution)/shard_map/scyp,cbiap->sbiya/dot_general | solution.py:53
  236.9 23.0 %copy.117 = f32[2,4,64,128,64]{4,3,2,1,0:T(8,128)} copy(f32[2,4,64,128,64]{3,4,0,2,1:T(8,128)} %fusion.76) | data formatting | bytes 33554432 | tf_op jit(solution)/shard_map/scyp,cbiap->sbiya/transpose | solution.py:53
  259.9 28.3 %reshape_reshape.6 = f32[2,256,32,256]{3,2,1,0:T(8,128)} reshape(f32[2,4,64,128,64]{4,3,2,1,0:T(8,128)} %copy.117) | data formatting | bytes 33554432 | tf_op jit(solution)/shard_map/reshape;reshape | solution.py:171
  291.5 3.5 fusion.114
  295.0 3.5 fusion.113
  301.9 3.5 fusion.111
  325.8 3.4 fusion.104
  329.2 3.5 fusion.103
  339.5 3.5 fusion.100
  353.2 3.5 fusion.96
  356.7 3.5 fusion.95
  367.0 3.5 fusion.92
  377.2 3.6 fusion.89
  391.1 3.5 fusion.85
  398.0 5.0 all-to-all-start.3
  403.2 382.5 %all-to-all-done.3 = f32[32,2,256,1,256]{4,3,2,1,0:T(1,128)} async-done(((f32[32,2,256,1,256]{4,3,2,1,0:T(1,128)}), f32[32,2,256,1,256]{4,3,2,1,0:T(1,128)}, u32[]{:S(2)}, u32[]{:S(2)}) %all-to-all-start.3) | async-done | bytes 16777248 | tf_op jit(solution)/shard_map/all_to_all | solution.py:168
  785.7 12.7 %copy.118 = f32[2,32,256,1,256]{4,2,1,0,3:T(8,128)} copy(f32[2,32,256,1,256]{4,3,2,0,1:T(1,128)} %bitcast.91) | data formatting | bytes 33554432 | tf_op jit(solution)/shard_map/reshape | solution.py:167
  798.4 25.6 %fusion.78 = f32[2,64,128,256]{3,1,2,0:T(8,128)} fusion(f32[2,64,128,256]{3,2,1,0:T(8,128)} %bitcast.379, f32[1,2,64,64]{3,2,1,0:T(8,128)S(1)} %get-tuple-element.147, f32[1,2,64,64]{3,2,1,0:T(8,128)S(1)} %get-tuple-element.146), kind=kOutput, calls=%fused_computation.141 | convolution fusion | flops 3221241856 | bytes 33619968 | tf_op jit(solution)/shard_map/scaq,cqpy->sapy/dot_general | solution.py:64
  824.0 13.8 %multiply_subtract_fusion = (f32[1,64,128,256]{3,1,2,0:T(8,128)}, f32[1,64,128,256]{3,1,2,0:T(8,128)}) fusion(f32[2,64,128,256]{3,1,2,0:T(8,128)} %fusion.78, f32[64,128]{0,1:T(8,128)S(1)} %copy.121, f32[64,128]{0,1:T(8,128)S(1)} %copy.120), kind=kLoop, calls=%fused_computation.138 | loop fusion | flops 12582912 | bytes 33619968 | tf_op jit(solution)/shard_map/sub | solution.py:69
  837.8 6.7 pad_maximum_fusion.2
  844.5 14.3 %fusion.81 = f32[256,128,64]{0,1,2:T(8,128)} fusion(f32[2,64,128,256]{3,1,2,0:T(8,128)S(1)} %pad_maximum_fusion.2, f32[1,128,128]{2,1,0:T(8,128)S(1)} %fusion.144, f32[1,128,128]{2,1,0:T(8,128)S(1)} %get-tuple-element.153), kind=kOutput, calls=%fused_computation.142 | convolution fusion | flops 3221291008 | bytes 25296896 | tf_op jit(solution)/shard_map/cbp,capy->yba/dot_general | solution.py:74
  858.8 11.5 %copy.123 = f32[256,128,64]{0,2,1:T(8,128)} copy(f32[256,128,64]{0,1,2:T(8,128)} %fusion.81) | data formatting | bytes 16777216 | tf_op jit(solution)/shard_map/cbp,capy->yba/transpose | solution.py:74
  870.3 8.9 %copy.124 = f32[256,8192]{1,0:T(8,128)} copy(f32[256,8192]{0,1:T(8,128)} %bitcast.383) | data formatting | bytes 16777216 | tf_op jit(solution)/shard_map/reshape | solution.py:75
  (195 shorter events, 104.5 us)
Async XLA Ops:
  1.4 9.9 %all-to-all-start = ((s32[4,1,128]{2,1,0:T(1,128)}), s32[4,1,128]{2,1,0:T(1,128)S(1)}, u32[]{:S(2)}, u32[]{:S(2)}) async-start(s32[4,1,128]{2,1,0:T(1,128)} %reshape.439), calls=%async_computation | async-start | bytes 4096 | tf_op jit(solution)/shard_map/all_to_all | solution.py:144
  11.2 10.2 %all-to-all-start.1 = ((f32[4,4,32,2,128]{4,2,3,1,0:T(8,128)}), f32[4,4,32,2,128]{4,2,3,1,0:T(8,128)S(1)}, u32[]{:S(2)}, u32[]{:S(2)}) async-start(f32[4,4,32,2,128]{4,2,3,1,0:T(8,128)} %bitcast.32), calls=%async_computation.1 | async-start | bytes 1048576 | tf_op jit(solution)/shard_map/all_to_all | solution.py:129
  21.4 10.0 %all-to-all-start.2 = ((s32[4,4,32,2,128]{4,2,3,1,0:T(8,128)}), s32[4,4,32,2,128]{4,2,3,1,0:T(8,128)S(1)}, u32[]{:S(2)}, u32[]{:S(2)}) async-start(s32[4,4,32,2,128]{4,2,3,1,0:T(8,128)} %bitcast.36), calls=%async_computation.2 | async-start | bytes 1048576 | tf_op jit(solution)/shard_map/all_to_all | solution.py:137
  31.5 152.3 %copy-start.2 = (f32[1,64,64]{2,1,0:T(8,128)S(1)}, f32[1,64,64]{2,1,0:T(8,128)}, u32[]{:S(2)}) copy-start(f32[1,64,64]{2,1,0:T(8,128)} %get-tuple-element.148) | copy-start | bytes 49156
  31.5 152.3 %copy-start.3 = (f32[1,64,64]{2,1,0:T(8,128)S(1)}, f32[1,64,64]{2,1,0:T(8,128)}, u32[]{:S(2)}) copy-start(f32[1,64,64]{2,1,0:T(8,128)} %get-tuple-element.149) | copy-start | bytes 49156
  179.7 19.3 %collective-permute-start = (f32[64,2,8,128]{3,0,1,2:T(8,128)S(1)}, f32[64,2,8,128]{3,0,1,2:T(8,128)S(1)}, u32[]{:S(2)}, u32[]{:S(2)}) collective-permute-start(f32[64,2,8,128]{3,0,1,2:T(8,128)S(1)} %slice_bitcast_fusion.39), channel_id=1, source_target_pairs={{0,1},{1,2},{2,3},{3,4},{4,5},{5,6},{6,7},{7,8},{8,9},{9,10},{10,1... | collective-permute-start | bytes 1572872 | tf_op jit(solution)/shard_map/ppermute | solution.py:16
  201.0 13.5 %copy-start = (f32[64,128]{1,0:T(8,128)S(1)}, f32[64,128]{1,0:T(8,128)}, u32[]{:S(2)}) copy-start(f32[64,128]{1,0:T(8,128)} %get-tuple-element.150) | copy-start | bytes 98308
  201.0 13.5 %copy-start.1 = (f32[64,128]{1,0:T(8,128)S(1)}, f32[64,128]{1,0:T(8,128)}, u32[]{:S(2)}) copy-start(f32[64,128]{1,0:T(8,128)} %get-tuple-element.151) | copy-start | bytes 98308
  398.0 387.7 %all-to-all-start.3 = ((f32[32,2,256,1,256]{4,3,2,1,0:T(1,128)}), f32[32,2,256,1,256]{4,3,2,1,0:T(1,128)}, u32[]{:S(2)}, u32[]{:S(2)}) async-start(f32[32,2,256,1,256]{4,3,2,1,0:T(1,128)} %fusion.84), calls=%async_computation.3 | async-start | bytes 33554432 | tf_op jit(solution)/shard_map/all_to_all | solution.py:168
